TPU v7x, 32 devices: a whole 2x2x4 slice. The times are simulated.
32 devices in a mesh: lat: 8 (over z, y), grp: 4 (over x, core).
Axes of the slice: x: 2, y: 2, z: 4, core: 2. Of those that a mesh axis runs over, the one named last changes fastest.
Arguments:
- tokens: bfloat16 [384, 64, 1024], P('grp', 'lat'), may hold values from -6 to 6
- cotangent: bfloat16 [384, 64, 1024], P('grp', 'lat'), may hold values from -6 to 6
- gain: float32 [384], P('grp'), may hold values from 0.5 to 1.5
- shift: float32 [384], P('grp'), may hold values from -3 to 3
- w_in: float32 [4, 2, 96, 96], P('grp'), may hold values from -0.4375 to 0.4375
- b_in: float32 [4, 2, 96], P('grp'), may hold values from -0.3 to 0.3
- w_out: float32 [4, 2, 96, 96], P('grp'), may hold values from -0.4375 to 0.4375
- b_out: float32 [4, 2, 96], P('grp'), may hold values from -0.12 to 0.12
Outputs:
- mixed: bfloat16 [384, 64, 1024], P('grp', 'lat')
- grad_tokens: bfloat16 [384, 64, 1024], P('grp', 'lat')
- grad_weights: float32 [4, 36864], P('grp', 'lat')
All inputs are finite; a program needn't handle non-finite values.
Results may differ from a plain program's by a relative error of at most 0.012.
Values sent between devices are 32-bit elements; how exact they have to be, the bound alone decides.
A program may use at most 128 MiB of HBM per device.

v0:
```python
import math

import jax
import jax.numpy as jnp
from jax import lax
from jax.sharding import PartitionSpec as P

highest = lax.Precision.HIGHEST
shrink_level = 0.01
norm_eps = 1e-05


def contract(form, left, right):
    return jnp.einsum(form, left, right, precision=highest)


def angle_table(left_count, right_count, length):
    left_index = jnp.arange(left_count, dtype=jnp.int32)[:, None]
    right_index = jnp.arange(right_count, dtype=jnp.int32)[None, :]
    phase = left_index * right_index % length
    theta = phase.astype(jnp.float32) * (2.0 * math.pi / length)
    return (jnp.cos(theta), jnp.sin(theta))


def lon_forward(field, modes):
    length = field.shape[2]
    cos_tab, sin_tab = angle_table(length, modes, length)
    scale = 1.0 / math.sqrt(length)
    out_real = contract("crn,nm->cmr", field, cos_tab) * scale
    out_imag = contract("crn,nm->cmr", field, sin_tab) * -scale
    return jnp.stack([out_real, out_imag])


def lon_inverse(stack, length, weighted):
    modes = stack.shape[2]
    cos_tab, sin_tab = angle_table(modes, length, length)
    scale = 1.0 / math.sqrt(length)
    real_part = stack[0]
    imag_part = stack[1]
    if weighted:
        mode_weight = jnp.where(jnp.arange(modes) == 0, 1.0, 2.0).astype(jnp.float32)[None, :, None]
        real_part = real_part * mode_weight
        imag_part = imag_part * mode_weight
    out = contract("cmr,mn->crn", real_part, cos_tab) - contract("cmr,mn->crn", imag_part, sin_tab)
    return out * scale


def lat_forward(stack):
    real_part, imag_part = (stack[0], stack[1])
    length = real_part.shape[-1]
    cos_tab, sin_tab = angle_table(length, length, length)
    scale = 1.0 / math.sqrt(length)
    out_real = contract("cql,lk->cqk", real_part, cos_tab) + contract(
        "cql,lk->cqk", imag_part, sin_tab
    )
    out_imag = contract("cql,lk->cqk", imag_part, cos_tab) - contract(
        "cql,lk->cqk", real_part, sin_tab
    )
    return (out_real * scale, out_imag * scale)


def lat_inverse(real_part, imag_part):
    length = real_part.shape[-1]
    cos_tab, sin_tab = angle_table(length, length, length)
    scale = 1.0 / math.sqrt(length)
    out_real = contract("cql,lk->cqk", real_part, cos_tab) - contract(
        "cql,lk->cqk", imag_part, sin_tab
    )
    out_imag = contract("cql,lk->cqk", imag_part, cos_tab) + contract(
        "cql,lk->cqk", real_part, sin_tab
    )
    return jnp.stack([out_real * scale, out_imag * scale])


def complex_mix(left_real, left_imag, weight):
    form = "bihk,bio->bohk"
    w_real = weight[:, 0]
    w_imag = weight[:, 1]
    out_real = contract(form, left_real, w_real) - contract(form, left_imag, w_imag)
    out_imag = contract(form, left_imag, w_real) + contract(form, left_real, w_imag)
    return (out_real, out_imag)


def mix_back(grad_real, grad_imag, weight):
    form = "bohk,bio->bihk"
    w_real = weight[:, 0]
    w_imag = weight[:, 1]
    back_real = contract(form, grad_real, w_real) + contract(form, grad_imag, w_imag)
    back_imag = contract(form, grad_imag, w_real) - contract(form, grad_real, w_imag)
    return (back_real, back_imag)


def weight_grad(left_real, left_imag, grad_real, grad_imag):
    form = "bihk,bohk->bio"
    grad_wreal = contract(form, left_real, grad_real) + contract(form, left_imag, grad_imag)
    grad_wimag = contract(form, left_real, grad_imag) - contract(form, left_imag, grad_real)
    return (grad_wreal, grad_wimag)


def shrink(value):
    return jnp.sign(value) * jnp.maximum(jnp.abs(value) - shrink_level, 0.0)


def regroup_modes(parts, lat_count, grp_count):
    _, two, chans, quarter, rows = parts.shape
    split = parts.reshape(lat_count, grp_count, two, chans, quarter, rows)
    split = jnp.transpose(split, (2, 1, 3, 4, 0, 5))
    return split.reshape(two, grp_count * chans, quarter, lat_count * rows)


def regroup_rows(stack, lat_count, grp_count, chans):
    two, _, quarter, lat_len = stack.shape
    rows = lat_len // lat_count
    split = stack.reshape(two, grp_count, chans, quarter, lat_count, rows)
    split = jnp.transpose(split, (4, 1, 0, 2, 3, 5))
    return split.reshape(lat_count * grp_count, two, chans, quarter, rows)


def per_device(tokens, cotangent, gain, shift, w_in, b_in, w_out, b_out):
    chans, rows, length = tokens.shape
    lat_count = lax.axis_size("lat")
    grp_count = lax.axis_size("grp")
    all_chans = chans * grp_count
    modes = length // 2
    tok_val = tokens.astype(jnp.float32)
    grad_val = cotangent.astype(jnp.float32)
    first_sum, second_sum = lax.psum(
        (jnp.sum(tok_val, axis=0), jnp.sum(tok_val * tok_val, axis=0)), "grp"
    )
    token_mean = first_sum / all_chans
    inv_std = lax.rsqrt(second_sum / all_chans - token_mean * token_mean + norm_eps)
    normed = (tok_val - token_mean) * inv_std
    normal_out = normed * gain[:, None, None] + shift[:, None, None]
    mode_weight = jnp.where(jnp.arange(modes) == 0, 1.0, 2.0).astype(jnp.float32)[
        None, None, :, None
    ]
    spec_field = lon_forward(normal_out, modes)
    spec_grad = lon_forward(grad_val, modes) * mode_weight
    parts_field, parts_grad = (
        lax.all_to_all(spec_field[None], ("lat", "grp"), split_axis=3, concat_axis=0, tiled=True),
        lax.all_to_all(spec_grad[None], ("lat", "grp"), split_axis=3, concat_axis=0, tiled=True),
    )
    modes_field = regroup_modes(parts_field, lat_count, grp_count)
    modes_grad = regroup_modes(parts_grad, lat_count, grp_count)
    block_in, bias_in, block_out, bias_out = (
        lax.all_gather(w_in, "grp", axis=0, tiled=True),
        lax.all_gather(b_in, "grp", axis=0, tiled=True),
        lax.all_gather(w_out, "grp", axis=0, tiled=True),
        lax.all_gather(b_out, "grp", axis=0, tiled=True),
    )
    block_count = block_in.shape[0]
    block_size = block_in.shape[2]
    quarter = modes_field.shape[2]
    lat_len = modes_field.shape[3]
    spec_real, spec_imag = lat_forward(modes_field)
    grad_real, grad_imag = lat_forward(modes_grad)
    blocked = (block_count, block_size, quarter, lat_len)
    spec_real = spec_real.reshape(blocked)
    spec_imag = spec_imag.reshape(blocked)
    grad_real = grad_real.reshape(blocked)
    grad_imag = grad_imag.reshape(blocked)
    pre_real, pre_imag = complex_mix(spec_real, spec_imag, block_in)
    pre_real = pre_real + bias_in[:, 0, :, None, None]
    pre_imag = pre_imag + bias_in[:, 1, :, None, None]
    act_real = jax.nn.relu(pre_real)
    act_imag = jax.nn.relu(pre_imag)
    post_real, post_imag = complex_mix(act_real, act_imag, block_out)
    post_real = post_real + bias_out[:, 0, :, None, None]
    post_imag = post_imag + bias_out[:, 1, :, None, None]
    shrunk_real = shrink(post_real)
    shrunk_imag = shrink(post_imag)
    d_post_real = jnp.where(jnp.abs(post_real) > shrink_level, grad_real, 0.0)
    d_post_imag = jnp.where(jnp.abs(post_imag) > shrink_level, grad_imag, 0.0)
    g_out_real, g_out_imag = weight_grad(act_real, act_imag, d_post_real, d_post_imag)
    d_act_real, d_act_imag = mix_back(d_post_real, d_post_imag, block_out)
    d_pre_real = jnp.where(pre_real > 0.0, d_act_real, 0.0)
    d_pre_imag = jnp.where(pre_imag > 0.0, d_act_imag, 0.0)
    g_in_real, g_in_imag = weight_grad(spec_real, spec_imag, d_pre_real, d_pre_imag)
    d_spec_real, d_spec_imag = mix_back(d_pre_real, d_pre_imag, block_in)
    flat_shape = (block_count * block_size, quarter, lat_len)
    back_field = lat_inverse(shrunk_real.reshape(flat_shape), shrunk_imag.reshape(flat_shape))
    back_grad = lat_inverse(d_spec_real.reshape(flat_shape), d_spec_imag.reshape(flat_shape))
    grad_stack = jnp.stack([g_in_real, g_in_imag, g_out_real, g_out_imag], axis=1)
    grad_term = grad_stack.reshape(block_count, 4 * block_size * block_size) * (
        1.0 / math.sqrt(lat_len * modes)
    )
    send_field = regroup_rows(back_field, lat_count, grp_count, chans)
    send_grad = regroup_rows(back_grad, lat_count, grp_count, chans)
    rows_field, rows_grad = (
        lax.all_to_all(send_field, ("lat", "grp"), split_axis=0, concat_axis=3, tiled=True),
        lax.all_to_all(send_grad, ("lat", "grp"), split_axis=0, concat_axis=3, tiled=True),
    )
    rows_field = rows_field[0]
    rows_grad = rows_grad[0]
    piece = grad_term.shape[1] // lat_count
    ordered = jnp.transpose(grad_term.reshape(block_count, lat_count, piece), (1, 0, 2))
    grad_weights = lax.psum_scatter(
        ordered.reshape(lat_count * block_count, piece),
        ("lat", "grp"),
        scatter_dimension=0,
        tiled=True,
    )
    filtered = lon_inverse(rows_field, length, True)
    pulled = lon_inverse(rows_grad, length, False)
    mixed = (filtered + normal_out + tok_val).astype(jnp.bfloat16)
    d_normal = grad_val + pulled
    dnorm = d_normal * gain[:, None, None]
    back_one, back_two = lax.psum((jnp.sum(dnorm, axis=0), jnp.sum(dnorm * normed, axis=0)), "grp")
    grad_tokens = grad_val + inv_std * (
        dnorm - back_one / all_chans - normed * (back_two / all_chans)
    )
    return (mixed, grad_tokens.astype(jnp.bfloat16), grad_weights)


def solution(mesh):
    in_specs = (
        P("grp", "lat", None),
        P("grp", "lat", None),
        P("grp"),
        P("grp"),
        P("grp", None, None, None),
        P("grp", None, None),
        P("grp", None, None, None),
        P("grp", None, None),
    )
    out_specs = (P("grp", "lat", None), P("grp", "lat", None), P("grp", "lat"))
    return jax.shard_map(
        per_device, mesh=mesh, in_specs=in_specs, out_specs=out_specs, check_vma=False
    )
```

profile of v0, /device:TPU:0, one launch (start us, length us, event | category | flops | bytes accessed | tf_op | source)
XLA Modules:
  0.0 714.5 jit_solution(96283752565888602)
XLA Ops:
  7.2 12.5 %multiply_bitcast_fusion.2 = f32[1,1,96,512,8]{3,2,4,1,0:T(8,128)S(1)} fusion(bf16[96,8,1024]{2,1,0:T(8,128)(2,1)} %param.9), kind=kOutput, calls=%fused_computation.130 | convolution fusion | flops 4839571456 | bytes 3145728 | tf_op jit(solution)/shard_map/crn,nm->cmr/dot_general | solution.py:14
  19.7 11.2 %multiply_bitcast_fusion.3 = f32[1,1,96,512,8]{3,2,4,1,0:T(8,128)S(1)} fusion(bf16[96,8,1024]{2,1,0:T(8,128)(2,1)S(1)} %copy-done.30), kind=kOutput, calls=%fused_computation.131 | convolution fusion | flops 4839571456 | bytes 3145728 | tf_op jit(solution)/shard_map/crn,nm->cmr/dot_general | solution.py:14
  34.8 7.5 %all-to-all-start.2 = ((f32[1,2,96,512,8]{2,4,1,0,3:T(8,128)}), f32[1,2,96,512,8]{2,4,1,0,3:T(8,128)}, u32[]{:S(2)}, u32[]{:S(2)}) async-start(f32[1,2,96,512,8]{2,4,1,0,3:T(8,128)} %copy.115), calls=%async_computation.2 | async-start | bytes 8388608 | tf_op jit(solution)/shard_map/all_to_all | solution.py:141
  43.8 40.9 %all-reduce.11.cloned.1.call-done = (f32[8,1024]{1,0:T(8,128)}, f32[8,1024]{1,0:T(8,128)}) async-done(((f32[8,1024]{1,0:T(8,128)}, f32[8,1024]{1,0:T(8,128)}), (f32[8,1024]{1,0:T(8,128)}, f32[8,1024]{1,0:T(8,128)})) %all-reduce.11.cloned.1.call-update) | async-done | bytes 65552 | tf_op jit(solution)/shard_map/psum | solution.py:127
  86.7 14.0 %multiply_bitcast_fusion.4 = f32[1,96,512,8]{2,1,3,0:T(8,128)S(1)} fusion(f32[96,8,1024]{2,1,0:T(8,128)S(1)} %fusion.6), kind=kOutput, calls=%fused_computation.136 | convolution fusion | flops 4839571456 | bytes 4718592 | tf_op jit(solution)/shard_map/crn,nm->cmr/dot_general | solution.py:14
  100.7 14.1 %multiply_bitcast_fusion.5 = f32[1,96,512,8]{2,1,3,0:T(8,128)S(1)} fusion(f32[96,8,1024]{2,1,0:T(8,128)S(1)} %fusion.6), kind=kOutput, calls=%fused_computation.137 | convolution fusion | flops 4839571456 | bytes 4718592 | tf_op jit(solution)/shard_map/crn,nm->cmr/dot_general | solution.py:14
  118.7 17.3 %all-to-all-done.2 = f32[1,2,96,512,8]{2,4,1,0,3:T(8,128)} async-done(((f32[1,2,96,512,8]{2,4,1,0,3:T(8,128)}), f32[1,2,96,512,8]{2,4,1,0,3:T(8,128)}, u32[]{:S(2)}, u32[]{:S(2)}) %all-to-all-start.2) | async-done | bytes 3145760 | tf_op jit(solution)/shard_map/all_to_all | solution.py:141
  136.0 4.2 all-to-all-start
  140.2 27.9 %all_gather.13 = f32[4,2,96]{2,1,0:T(2,128)S(1)} all-gather(f32[1,2,96]{2,1,0:T(2,128)S(1)} %copy-done.39), channel_id=1, replica_groups=mesh['lat'=8,'grp'=4] {'grp'}, dimensions={0}, use_global_device_ids=true | all-gather | bytes 3840 | tf_op jit(solution)/shard_map/all_gather | solution.py:147
  168.1 5.7 all_gather.15
  173.8 6.7 all_gather.12
  180.5 13.8 %all_gather.14 = f32[4,2,96,96]{3,2,0,1:T(8,128)} all-gather(f32[1,2,96,96]{3,2,0,1:T(8,128)S(1)} %bitcast.375), channel_id=1, replica_groups=mesh['lat'=8,'grp'=4] {'grp'}, dimensions={0}, use_global_device_ids=true | all-gather | bytes 368640 | tf_op jit(solution)/shard_map/all_gather | solution.py:148
  194.9 4.9 copy.198
  221.4 12.5 %all-to-all-done = f32[1,2,96,512,8]{2,4,1,0,3:T(8,128)} async-done(((f32[1,2,96,512,8]{2,4,1,0,3:T(8,128)}), f32[1,2,96,512,8]{2,4,1,0,3:T(8,128)}, u32[]{:S(2)}, u32[]{:S(2)}) %all-to-all-start) | async-done | bytes 3145760 | tf_op jit(solution)/shard_map/all_to_all | solution.py:140
  233.9 4.9 copy.199
  274.0 3.8 copy_select_fusion
  284.5 6.5 copy_select_fusion.1
  323.2 4.6 all-to-all-start.1
  327.9 3.7 fusion.208
  349.9 3.7 fusion.28
  387.2 34.0 %all-to-all-done.1 = f32[32,2,96,16,8]{2,4,3,1,0:T(8,128)} async-done(((f32[32,2,96,16,8]{2,4,3,1,0:T(8,128)}), f32[32,2,96,16,8]{2,4,3,1,0:T(8,128)}, u32[]{:S(2)}, u32[]{:S(2)}) %all-to-all-start.1) | async-done | bytes 3145760 | tf_op jit(solution)/shard_map/all_to_all | solution.py:190
  421.2 4.2 all-to-all-start.3
  425.9 5.8 fusion.127
  449.4 3.7 fusion.183
  458.5 143.4 %all-reduce.7.cloned.1.call-done = f32[32,4608]{1,0:T(8,128)} async-done(((f32[32,4608]{1,0:T(8,128)}), f32[32,4608]{1,0:T(8,128)}) %all-reduce.7.cloned.1.call-update) | async-done | bytes 589840
  613.5 15.6 %fusion.40 = f32[96,8,1024]{2,1,0:T(8,128)} fusion(f32[96,512,8]{1,2,0:T(8,128)} %copy.112), kind=kOutput, calls=%fused_computation.58 | convolution fusion | flops 4839178240 | bytes 4718592 | tf_op jit(solution)/shard_map/cmr,mn->crn/dot_general | solution.py:14
  629.1 3.9 fusion.364
  637.9 16.3 %fusion.38 = f32[96,8,1024]{2,1,0:T(8,128)S(1)} fusion(f32[96,512,8]{1,2,0:T(8,128)} %copy.125), kind=kOutput, calls=%fused_computation.56 | convolution fusion | flops 4839178240 | bytes 4718592 | tf_op jit(solution)/shard_map/cmr,mn->crn/dot_general | solution.py:14
  654.3 16.1 %fusion.363 = (f32[8,1024]{1,0:T(8,128)}, f32[8,1024]{1,0:T(8,128)}, f32[96,8,1024]{2,1,0:T(8,128)}) fusion(f32[8,1024]{1,0:T(8,128)S(1)} %copy-done.35, f32[8,1024]{1,0:T(8,128)S(1)} %copy-done.33, bf16[96,8,1024]{2,1,0:T(8,128)(2,1)S(1)} %copy-done.23, f32[96]{0:T(128)S(1)} %copy-done.44, f32[96,8,1024]{2,1,0:T(8,128)S(1)} %fusion.38, ...), kind=kOutput, calls=%fused_computation.321 | convolution fusion | flops 4847812608 | bytes 11141504 | tf_op jit(solution)/shard_map/cmr,mn->crn/dot_general | solution.py:14
  670.4 16.2 %fusion.11 = bf16[96,8,1024]{2,1,0:T(8,128)(2,1)} fusion(bf16[96,8,1024]{2,1,0:T(8,128)(2,1)S(1)} %copy-done.23, f32[96,8,1024]{2,1,0:T(8,128)} %fusion.40, f32[96,512,8]{1,2,0:T(8,128)S(1)} %copy-done.28, f32[96]{0:T(128)S(1)} %copy-done.42, f32[96]{0:T(128)S(1)} %copy-done.44, f32[8,1024]{1,0:T(8,128)S(1)} %copy-done.35, f32[8,1024]{1,0:T(8,128)S(1)} %copy-done.33), kind=kOutput, calls=%fused_computation.21 | convolution fusion | flops 4847042560 | bytes 7930624 | tf_op jit(solution)/shard_map/cmr,mn->crn/dot_general | solution.py:14
  686.6 15.8 %all-reduce.9.cloned.1.call-done = (f32[8,1024]{1,0:T(8,128)}, f32[8,1024]{1,0:T(8,128)}) async-done(((f32[8,1024]{1,0:T(8,128)}, f32[8,1024]{1,0:T(8,128)}), (f32[8,1024]{1,0:T(8,128)}, f32[8,1024]{1,0:T(8,128)})) %all-reduce.9.cloned.1.call-update) | async-done | bytes 65552 | tf_op jit(solution)/shard_map/psum | solution.py:208
  703.2 4.5 fusion.1
  (184 shorter events, 199.6 us)
Async XLA Ops:
  7.2 12.5 %copy-start.30 = (bf16[96,8,1024]{2,1,0:T(8,128)(2,1)S(1)}, bf16[96,8,1024]{2,1,0:T(8,128)(2,1)}, u32[]{:S(2)}) copy-start(bf16[96,8,1024]{2,1,0:T(8,128)(2,1)} %param.9) | copy-start | bytes 4718596
  34.8 7.9 %copy-start.22 = (bf16[96,8,1024]{2,1,0:T(8,128)(2,1)S(1)}, bf16[96,8,1024]{2,1,0:T(8,128)(2,1)}, u32[]{:S(2)}) copy-start(bf16[96,8,1024]{2,1,0:T(8,128)(2,1)} %param.8) | copy-start | bytes 4718596
  34.8 51.4 %copy-start.41 = (f32[96]{0:T(128)S(1)}, f32[96]{0:T(128)}, u32[]{:S(2)}) copy-start(f32[96]{0:T(128)} %param.11) | copy-start | bytes 1156
  34.8 51.4 %copy-start.43 = (f32[96]{0:T(128)S(1)}, f32[96]{0:T(128)}, u32[]{:S(2)}) copy-start(f32[96]{0:T(128)} %param.10) | copy-start | bytes 1156
  34.8 101.2 %all-to-all-start.2 = ((f32[1,2,96,512,8]{2,4,1,0,3:T(8,128)}), f32[1,2,96,512,8]{2,4,1,0,3:T(8,128)}, u32[]{:S(2)}, u32[]{:S(2)}) async-start(f32[1,2,96,512,8]{2,4,1,0,3:T(8,128)} %copy.115), calls=%async_computation.2 | async-start | bytes 8388608 | tf_op jit(solution)/shard_map/all_to_all | solution.py:141
  42.3 42.5 %all-reduce.11.cloned.1.call-start = ((), (), s32[]{:S(2)}) async-start(), calls=%async_computation.6 | async-start | bytes 131072 | tf_op jit(solution)/shard_map/psum | solution.py:127
  118.7 21.6 %copy-start.39 = (f32[1,2,96]{2,1,0:T(2,128)S(1)}, f32[1,2,96]{2,1,0:T(2,128)}, u32[]{:S(2)}) copy-start(f32[1,2,96]{2,1,0:T(2,128)} %param.13) | copy-start | bytes 2308
  118.7 49.5 %copy-start.40 = (f32[1,2,96]{2,1,0:T(2,128)S(1)}, f32[1,2,96]{2,1,0:T(2,128)}, u32[]{:S(2)}) copy-start(f32[1,2,96]{2,1,0:T(2,128)} %param.15) | copy-start | bytes 2308
  118.7 55.1 %copy-start.36 = (f32[1,2,96,96]{3,2,1,0:T(8,128)S(1)}, f32[1,2,96,96]{3,2,1,0:T(8,128)}, u32[]{:S(2)}) copy-start(f32[1,2,96,96]{3,2,1,0:T(8,128)} %param.12) | copy-start | bytes 221188
  118.7 61.8 %copy-start.37 = (f32[1,2,96,96]{3,2,1,0:T(8,128)S(1)}, f32[1,2,96,96]{3,2,1,0:T(8,128)}, u32[]{:S(2)}) copy-start(f32[1,2,96,96]{3,2,1,0:T(8,128)} %param.14) | copy-start | bytes 221188
  136.0 97.9 %all-to-all-start = ((f32[1,2,96,512,8]{2,4,1,0,3:T(8,128)}), f32[1,2,96,512,8]{2,4,1,0,3:T(8,128)}, u32[]{:S(2)}, u32[]{:S(2)}) async-start(f32[1,2,96,512,8]{2,4,1,0,3:T(8,128)} %copy.98), calls=%async_computation | async-start | bytes 8388608 | tf_op jit(solution)/shard_map/all_to_all | solution.py:140
  274.0 3.8 copy-start
  323.2 97.9 %all-to-all-start.1 = ((f32[32,2,96,16,8]{2,4,3,1,0:T(8,128)}), f32[32,2,96,16,8]{2,4,3,1,0:T(8,128)}, u32[]{:S(2)}, u32[]{:S(2)}) async-start(f32[32,2,96,16,8]{2,4,3,1,0:T(8,128)} %bitcast.368), calls=%async_computation.1 | async-start | bytes 8388608 | tf_op jit(solution)/shard_map/all_to_all | solution.py:190
  327.9 3.7 copy-start.15
  349.9 3.7 copy-start.9
  421.2 207.9 %all-to-all-start.3 = ((f32[32,2,96,16,8]{2,4,3,1,0:T(8,128)}), f32[32,2,96,16,8]{2,4,3,1,0:T(8,128)}, u32[]{:S(2)}, u32[]{:S(2)}) async-start(f32[32,2,96,16,8]{2,4,3,1,0:T(8,128)} %bitcast.367), calls=%async_computation.3 | async-start | bytes 8388608 | tf_op jit(solution)/shard_map/all_to_all | solution.py:191
  425.4 176.5 %all-reduce.7.cloned.1.call-start = ((), (), s32[]{:S(2)}) async-start(), calls=%async_computation.4 | async-start | bytes 1179648
  425.9 5.9 copy-start.2
  425.9 5.9 copy-start.16
  431.8 3.5 copy-start.4
  431.8 3.5 copy-start.10
  442.4 3.5 copy-start.14
  445.9 3.5 copy-start.12
  458.5 243.9 %all-reduce.9.cloned.1.call-start = ((), (), s32[]{:S(2)}) async-start(), calls=%async_computation.5 | async-start | bytes 131072 | tf_op jit(solution)/shard_map/psum | solution.py:208
  637.9 16.3 %copy-start.23 = (bf16[96,8,1024]{2,1,0:T(8,128)(2,1)S(1)}, bf16[96,8,1024]{2,1,0:T(8,128)(2,1)}, u32[]{:S(2)}) copy-start(bf16[96,8,1024]{2,1,0:T(8,128)(2,1)} %param.8) | copy-start | bytes 4718596
  637.9 16.3 %copy-start.29 = (f32[96,512,8]{1,2,0:T(8,128)S(1)}, f32[96,512,8]{1,2,0:T(8,128)}, u32[]{:S(2)}) copy-start(f32[96,512,8]{1,2,0:T(8,128)} %copy.124) | copy-start | bytes 4718596
  637.9 16.3 %copy-start.31 = (bf16[96,8,1024]{2,1,0:T(8,128)(2,1)S(1)}, bf16[96,8,1024]{2,1,0:T(8,128)(2,1)}, u32[]{:S(2)}) copy-start(bf16[96,8,1024]{2,1,0:T(8,128)(2,1)} %param.9) | copy-start | bytes 4718596
  637.9 16.4 %copy-start.33 = (f32[8,1024]{1,0:T(8,128)S(1)}, f32[8,1024]{1,0:T(8,128)}, u32[]{:S(2)}) copy-start(f32[8,1024]{1,0:T(8,128)} %copy-done.32) | copy-start | bytes 98308
  637.9 16.4 %copy-start.35 = (f32[8,1024]{1,0:T(8,128)S(1)}, f32[8,1024]{1,0:T(8,128)}, u32[]{:S(2)}) copy-start(f32[8,1024]{1,0:T(8,128)} %copy-done.34) | copy-start | bytes 98308
  637.9 16.4 %copy-start.44 = (f32[96]{0:T(128)S(1)}, f32[96]{0:T(128)}, u32[]{:S(2)}) copy-start(f32[96]{0:T(128)} %param.10) | copy-start | bytes 1156
  654.3 16.1 %copy-start.28 = (f32[96,512,8]{1,2,0:T(8,128)S(1)}, f32[96,512,8]{1,2,0:T(8,128)}, u32[]{:S(2)}) copy-start(f32[96,512,8]{1,2,0:T(8,128)} %copy.111) | copy-start | bytes 4718596
  654.3 16.1 %copy-start.42 = (f32[96]{0:T(128)S(1)}, f32[96]{0:T(128)}, u32[]{:S(2)}) copy-start(f32[96]{0:T(128)} %param.11) | copy-start | bytes 1156
  (20 other events, 45.6 us)
Sparse Core Ops, SparseCore 0:
  46.0 38.6 all-reduce.10
  458.6 143.2 all-reduce.6
  670.5 31.8 all-reduce.8
where the time goes:
time: 724 us; the launch traced here: 714 us
  waiting for transfers between devices  264 us (36%)
  matrix products  227 us (31%)
  local copies, waits for them, and re-layouts  115 us (16%)
  blocking collectives  54.1 us (7%)
  starting transfers between devices  21.5 us (3%)
  other arithmetic  17.5 us (2%)
  between operations  14.9 us (2%)
    dot_general x48, matrix products, contract(): return jnp.einsum(form, left, right, precision=highest)  227 us
    unnamed x4, waiting for transfers between devices  143 us
    psum x1, waiting for transfers between devices, per_device(): lax.psum((jnp.sum(tok_val, axis=0), jnp.sum(tok_val * tok_val, axis=0)),...  40.9 us
    all_to_all x1, waiting for transfers between devices, per_device(): lax.all_to_all(send_field, ('lat', 'grp'), split_axis=0, concat_axis=3, t...  34 us
    all_gather x1, blocking collectives, per_device(): lax.all_gather(b_in, 'grp', axis=0, tiled=True)  27.9 us
    another operation x8, local copies, waits for them, and re-layouts, lat_inverse(): return jnp.stack([out_real * scale, out_imag * scale])  24.5 us
    all_to_all x1, waiting for transfers between devices, per_device(): lax.all_to_all(spec_grad[None], ('lat', 'grp'), split_axis=3, concat_axis...  17.3 us
    psum x1, waiting for transfers between devices, per_device(): lax.psum((jnp.sum(dnorm, axis=0), jnp.sum(dnorm * normed, axis=0)), 'grp')  15.8 us
  transfers between devices with their start and end apart: 7, of which 6 were waited for; matrix products, arithmetic and copies ran while one was open for 27% of the time, Pallas kernels for 0%

commit v1 on v0

v1 whole, which is shorter than its diff:
```python
import math

import numpy as np
import jax
import jax.numpy as jnp
from jax import lax
from jax.sharding import PartitionSpec as P

shrink_level = 0.01
norm_eps = 1e-05


precise = lax.Precision.HIGH


def contract(form, left, right):
    return jnp.einsum(form, left, right, precision=precise, preferred_element_type=jnp.float32)


def angles(left_count, right_count, length):
    phase = np.arange(left_count)[:, None] * np.arange(right_count)[None, :] % length
    theta = phase * (2.0 * math.pi / length)
    return np.cos(theta), np.sin(theta)


def lon_table(length, modes, owners):
    cos_tab, sin_tab = angles(length, modes, length)
    both = np.stack([cos_tab, -sin_tab]) / math.sqrt(length)
    both = both.reshape(2, length, owners, modes // owners)
    return both.transpose(1, 2, 0, 3).astype(np.float32)


def lat_table(length):
    cos_tab, sin_tab = angles(length, length, length)
    table = np.stack([np.stack([cos_tab, -sin_tab]), np.stack([sin_tab, cos_tab])])
    return (table / math.sqrt(length)).transpose(2, 0, 3, 1).astype(np.float32)


def group_sum(value, name):
    count = lax.axis_size(name)
    total = value
    for step in range(1, count):
        pairs = [(at, (at + step) % count) for at in range(count)]
        total = total + lax.ppermute(value, name, pairs)
    return total


def swap(value):
    return lax.all_to_all(value, "lat", split_axis=0, concat_axis=0, tiled=True)


def mix_matrix(weight):
    real_part, imag_part = weight[0], weight[1]
    top = jnp.stack([real_part, imag_part], axis=1)
    low = jnp.stack([-imag_part, real_part], axis=1)
    return jnp.stack([top, low])


def shrink(value):
    return jnp.sign(value) * jnp.maximum(jnp.abs(value) - shrink_level, 0.0)


def matrix_grad(full):
    real_part = full[0, :, 0] + full[1, :, 1]
    imag_part = full[0, :, 1] - full[1, :, 0]
    return real_part, imag_part


def per_device(tokens, cotangent, gain, shift, w_in, b_in, w_out, b_out):
    chans, rows, length = tokens.shape
    lat_count = lax.axis_size("lat")
    all_chans = chans * lax.axis_size("grp")
    modes = length // 2
    own = modes // lat_count
    lat_len = rows * lat_count
    table = lon_table(length, modes, lat_count).reshape(length, 2 * modes)
    table = jnp.asarray(table)
    lat_tab = jnp.asarray(lat_table(lat_len)).reshape(lat_count, rows, 2, lat_len, 2)
    tok_val = tokens.astype(jnp.float32)
    grad_val = cotangent.astype(jnp.float32)

    def lon_send(field):
        out = jnp.einsum("crn,ndq->dcrq", field, table.reshape(length, lat_count, 2 * own),
                         precision=precise, preferred_element_type=jnp.float32)
        return swap(out.reshape(lat_count, chans * rows, 2 * own))

    def lat_in(parts):
        parts = parts.reshape(lat_count, chans, rows, 2, own)
        return contract("scrim,srikj->kmjc", parts, lat_tab)

    def lat_out(value):
        out = contract("kmjc,srikj->scrim", value, lat_tab)
        return swap(out.reshape(lat_count, chans * rows, 2 * own))

    def lon_back(parts):
        parts = parts.reshape(lat_count, chans, rows, 2 * own)
        return contract("dcrq,ndq->crn", parts, table.reshape(length, lat_count, 2 * own))

    sums = jnp.stack([jnp.sum(tok_val, axis=0), jnp.sum(tok_val * tok_val, axis=0)])
    sums = group_sum(sums, "grp")
    token_mean = sums[0] / all_chans
    inv_std = lax.rsqrt(sums[1] / all_chans - token_mean * token_mean + norm_eps)
    normed = (tok_val - token_mean) * inv_std
    normal_out = normed * gain[:, None, None] + shift[:, None, None]
    recv_field = lon_send(normal_out)
    recv_grad = lon_send(grad_val)

    mat_in, mat_out = mix_matrix(w_in[0]), mix_matrix(w_out[0])
    at_mode = lax.axis_index("lat") * own + jnp.arange(own)
    mode_weight = jnp.where(at_mode == 0, 1.0, 2.0).astype(jnp.float32)[None, :, None, None]
    spec = lat_in(recv_field)
    pre = contract("kmic,icjo->kmjo", spec, mat_in) + b_in[0]
    act = jax.nn.relu(pre)
    post = contract("kmic,icjo->kmjo", act, mat_out) + b_out[0]
    rows_field = lat_out(shrink(post) * mode_weight)

    grad = lat_in(recv_grad) * mode_weight
    d_post = jnp.where(jnp.abs(post) > shrink_level, grad, 0.0)
    d_act = contract("kmjo,icjo->kmic", d_post, mat_out)
    d_pre = jnp.where(pre > 0.0, d_act, 0.0)
    d_spec = contract("kmjo,icjo->kmic", d_pre, mat_in)
    rows_grad = lat_out(d_spec)
    full_out = contract("kmic,kmjo->icjo", act, d_post)
    full_in = contract("kmic,kmjo->icjo", spec, d_pre)
    grads = jnp.stack([*matrix_grad(full_in), *matrix_grad(full_out)])
    grads = grads.reshape(lat_count, -1) * (1.0 / math.sqrt(lat_len * modes))
    grad_weights = jnp.sum(swap(grads), axis=0, keepdims=True)

    mixed = (lon_back(rows_field) + normal_out + tok_val).astype(jnp.bfloat16)
    dnorm = (grad_val + lon_back(rows_grad)) * gain[:, None, None]
    back = group_sum(jnp.stack([jnp.sum(dnorm, axis=0), jnp.sum(dnorm * normed, axis=0)]), "grp")
    grad_tokens = grad_val + inv_std * (
        dnorm - back[0] / all_chans - normed * (back[1] / all_chans)
    )
    return (mixed, grad_tokens.astype(jnp.bfloat16), grad_weights)


def solution(mesh):
    in_specs = (
        P("grp", "lat", None),
        P("grp", "lat", None),
        P("grp"),
        P("grp"),
        P("grp", None, None, None),
        P("grp", None, None),
        P("grp", None, None, None),
        P("grp", None, None),
    )
    out_specs = (P("grp", "lat", None), P("grp", "lat", None), P("grp", "lat"))
    return jax.shard_map(
        per_device, mesh=mesh, in_specs=in_specs, out_specs=out_specs, check_vma=False
    )
```

time: 724 us -> 430 us (0.59)
  matrix products: 227 us -> 109 us
  blocking collectives: 54.1 us -> 0 us
  waiting for transfers between devices: 264 us -> 210 us
  local copies, waits for them, and re-layouts: 115 us -> 67.9 us
  other arithmetic: 17.5 us -> 2.99 us
  between operations: 14.9 us -> 1.47 us
  starting transfers between devices: 21.5 us -> 30.6 us
    unnamed x4 -> x0, waiting for transfers between devices: 143 us -> none
    all_to_all x4 -> x5, waiting for transfers between devices: 63.9 us -> 206 us  [swap(): return lax.all_to_all(value, 'lat', split_axis=0, concat_axis=0, tiled=True)]
    dot_general x48 -> x14, matrix products: 227 us -> 109 us  [the longest x12 95.2 us: contract(): jnp.einsum(form, left, right, precision=precise, preferred_element_type=j...]
    psum x2 -> x0, waiting for transfers between devices: 56.7 us -> none  [the longest x1 40.9 us: per_device(): lax.psum((jnp.sum(tok_val, axis=0), jnp.sum(tok_val * tok_val, axis=0)),...]
    all_gather x4 -> x0, blocking collectives: 54.1 us -> none  [the longest x1 27.9 us: per_device(): lax.all_gather(b_in, 'grp', axis=0, tiled=True)]
    another operation x8 -> x2, local copies, waits for them, and re-layouts: 24.5 us -> 0.02 us  [mix_matrix(): top = jnp.stack([real_part, imag_part], axis=1)]
    transpose x1 -> x4, local copies, waits for them, and re-layouts: 0.38 us -> 21.8 us  [the longest x2 16.5 us: contract(): jnp.einsum(form, left, right, precision=precise, preferred_element_type=j...]
    squeeze x6 -> x0, local copies, waits for them, and re-layouts: 14.4 us -> none  [the longest x4 9.57 us: lat_forward(): real_part, imag_part = (stack[0], stack[1])]
  transfers between devices with their start and end apart: 7 -> 11, of which waited for: 6 -> 7; matrix products, arithmetic and copies ran while one was open for 27% -> 23% of each run, Pallas kernels for 0% -> 0%
where the time goes in v1:
time: 430 us; the launch traced here: 422 us
  waiting for transfers between devices  210 us (49%)
  matrix products  109 us (25%)
  local copies, waits for them, and re-layouts  67.9 us (16%)
  starting transfers between devices  30.6 us (7%)
    all_to_all x5, waiting for transfers between devices, swap(): return lax.all_to_all(value, 'lat', split_axis=0, concat_axis=0, tiled=True)  206 us
    dot_general x12, matrix products, contract(): jnp.einsum(form, left, right, precision=precise, preferred_element_type=j...  95.2 us
    reshape x4, local copies, waits for them, and re-layouts, lat_in(): parts = parts.reshape(lat_count, chans, rows, 2, own)  30.4 us
    all_to_all x5, starting transfers between devices, swap(): return lax.all_to_all(value, 'lat', split_axis=0, concat_axis=0, tiled=True)  26.5 us
    transpose x2, local copies, waits for them, and re-layouts, contract(): jnp.einsum(form, left, right, precision=precise, preferred_element_type=j...  16.5 us
    dot_general x2, matrix products, lon_send(): jnp.einsum('crn,ndq->dcrq', field, table.reshape(length, lat_count, 2 * o...  14.3 us
    reshape x2, local copies, waits for them, and re-layouts, lat_out(): return swap(out.reshape(lat_count, chans * rows, 2 * own))  14.2 us
  transfers between devices with their start and end apart: 11, of which 7 were waited for; matrix products, arithmetic and copies ran while one was open for 23% of the time, Pallas kernels for 0%

profile of v1, /device:TPU:0, one launch (start us, length us, event | category | flops | bytes accessed | tf_op | source)
XLA Modules:
  0.0 422.4 jit_solution(6649613110939162291)
XLA Ops:
  0.6 6.8 %convolution_bitcast_fusion.2 = f32[8,96,8,128]{3,1,2,0:T(8,128)S(1)} fusion(f32[1024,8,128,1]{2,0,3,1:T(8,128)} %constant.49, bf16[96,8,1024]{2,1,0:T(8,128)(2,1)} %param.11), kind=kOutput, calls=%fused_computation.63 | convolution fusion | flops 4831838208 | bytes 8912896 | tf_op jit(solution)/shard_map/crn,ndq->dcrq/dot_general | solution.py:83
  7.4 3.4 copy.150
  10.9 7.4 %all-to-all-start.2 = ((f32[8,768,128]{2,1,0:T(8,128)}), f32[8,768,128]{2,1,0:T(8,128)}, u32[]{:S(2)}, u32[]{:S(2)}) async-start(f32[8,768,128]{2,1,0:T(8,128)} %bitcast.220), calls=%async_computation.2 | async-start | bytes 6291456 | tf_op jit(solution)/shard_map/all_to_all | solution.py:49
  20.8 2.3 collective-permute-done.1
  24.6 7.5 %fusion.54 = f32[8,96,8,128]{3,2,0,1:T(8,128)S(1)} fusion(f32[1024,8,128,1]{2,0,1,3:T(8,128)} %constant.45, bf16[96,8,1024]{2,1,0:T(8,128)(2,1)S(1)} %copy-done.2, f32[96]{0:T(128)S(1)} %copy-done.13, f32[96]{0:T(128)S(1)} %copy-done.11, f32[8,1024]{1,0:T(8,128)S(1)} %get-tuple-element.20, f32[8,1024]{1,0:T(8,128)S(1)} %get-tuple-element.19), kind=kOutput, calls=%fused_computation.62 | convolution fusion | flops 4835770368 | bytes 8979200 | tf_op jit(solution)/shard_map/crn,ndq->dcrq/dot_general | solution.py:83
  33.9 55.2 %all-to-all-done.2 = f32[8,768,128]{2,1,0:T(8,128)} async-done(((f32[8,768,128]{2,1,0:T(8,128)}), f32[8,768,128]{2,1,0:T(8,128)}, u32[]{:S(2)}, u32[]{:S(2)}) %all-to-all-start.2) | async-done | bytes 3145760 | tf_op jit(solution)/shard_map/all_to_all | solution.py:49
  89.1 4.7 %all-to-all-start = ((f32[8,768,128]{2,1,0:T(8,128)}), f32[8,768,128]{2,1,0:T(8,128)}, u32[]{:S(2)}, u32[]{:S(2)}) async-start(f32[8,768,128]{2,1,0:T(8,128)} %bitcast.219), calls=%async_computation | async-start | bytes 6291456 | tf_op jit(solution)/shard_map/all_to_all | solution.py:49
  94.0 7.1 %reshape.173 = f32[8,96,8,2,64]{4,3,2,1,0:T(2,128)} reshape(f32[8,768,128]{2,1,0:T(8,128)} %all-to-all-done.2) | data formatting | bytes 6291456 | tf_op jit(solution)/shard_map/reshape | solution.py:88
  101.1 8.1 %copy.79 = f32[8,96,8,2,64,1]{1,0,2,3,5,4:T(8,128)} copy(f32[8,96,8,2,64,1]{4,3,2,1,0,5:T(2,128)} %bitcast.217) | data formatting | bytes 6291456 | tf_op jit(solution)/shard_map/reshape | solution.py:88
  109.2 6.1 %convolution_bitcast_fusion = f32[96,64,64,2]{0,2,3,1:T(8,128)} fusion(f32[8,96,8,2,64,1]{1,0,2,3,5,4:T(8,128)} %copy.79, f32[8,8,2,64,2,1]{3,0,1,2,4,5:T(8,128)S(1)} %copy-done.6), kind=kOutput, calls=%fused_computation.58 | convolution fusion | flops 603979776 | bytes 6356992 | tf_op jit(solution)/shard_map/scrim,srikj->kmjc/dot_general | solution.py:17
  115.3 48.7 %all-to-all-done = f32[8,768,128]{2,1,0:T(8,128)} async-done(((f32[8,768,128]{2,1,0:T(8,128)}), f32[8,768,128]{2,1,0:T(8,128)}, u32[]{:S(2)}, u32[]{:S(2)}) %all-to-all-start) | async-done | bytes 3145760 | tf_op jit(solution)/shard_map/all_to_all | solution.py:49
  164.0 7.1 %reshape.168 = f32[8,96,8,2,64]{4,3,2,1,0:T(2,128)} reshape(f32[8,768,128]{2,1,0:T(8,128)} %all-to-all-done) | data formatting | bytes 6291456 | tf_op jit(solution)/shard_map/reshape | solution.py:88
  171.1 8.1 %copy.70 = f32[8,96,8,2,64,1]{1,0,2,3,5,4:T(8,128)} copy(f32[8,96,8,2,64,1]{4,3,2,1,0,5:T(2,128)} %bitcast.218) | data formatting | bytes 6291456 | tf_op jit(solution)/shard_map/reshape | solution.py:88
  179.2 4.2 convolution_bitcast_fusion.1
  183.4 4.2 fusion.16
  187.6 18.5 %bitcast_select_fusion.1 = (f32[64,64,2,96]{3,1,2,0:T(8,128)S(1)}, f32[64,64,2,96,1,1]{3,1,2,0,5,4:T(8,128)}) fusion(f32[96,64,64,2]{0,2,3,1:T(8,128)S(1)} %copy-done.1, f32[64]{0:T(128)S(1)} %compare_select_fusion, f32[2,96]{1,0:T(2,128)S(1)} %bitcast.232, f32[1,96,2,96]{3,1,0,2:T(8,128)S(1)} %get-tuple-element.22, ...), kind=kOutput, calls=%fused_computation.19 | convolution fusion | flops 915443712 | bytes 12732160 | tf_op jit(solution)/shard_map/kmic,icjo->kmjo/dot_general | solution.py:17
  206.1 3.7 fusion.72
  211.8 7.0 %fusion.67 = f32[2,96,2,96]{3,1,2,0:T(8,128)S(1)} fusion(f32[64,64,2,96]{3,1,2,0:T(8,128)S(1)} %bitcast_select_fusion, f32[64,64,2,96,1]{3,0,2,1,4:T(8,128)S(1)} %convolution_bitcast_fusion.1), kind=kOutput, calls=%fused_computation.70 | convolution fusion | flops 905969664 | bytes 6438912 | tf_op jit(solution)/shard_map/kmic,kmjo->icjo/dot_general | solution.py:17
  219.8 13.7 %fusion.12 = f32[64,64,2,96,1]{3,0,4,2,1:T(8,128)} fusion(f32[64,64,2,96,1]{3,1,2,0,4:T(8,128)} %bitcast.216, f32[1,96,2,96]{3,1,0,2:T(8,128)S(1)} %get-tuple-element.24, f32[1,96,2,96]{3,1,0,2:T(8,128)S(1)} %get-tuple-element.23), kind=kOutput, calls=%fused_computation.16 | convolution fusion | flops 906006528 | bytes 6438912 | tf_op jit(solution)/shard_map/kmjo,icjo->kmic/dot_general | solution.py:17
  233.5 3.6 all-to-all-start.4
  237.1 6.1 %fusion.49 = f32[8,96,8,2,64]{1,2,3,0,4:T(8,128)} fusion(f32[8,8,2,64,2,1]{3,1,4,2,0,5:T(8,128)S(1)} %copy-done.5, f32[64,64,2,96,1]{3,0,4,2,1:T(8,128)} %fusion.12), kind=kOutput, calls=%fused_computation.57 | convolution fusion | flops 603979776 | bytes 6356992 | tf_op jit(solution)/shard_map/kmjc,srikj->scrim/dot_general | solution.py:17
  243.2 8.3 %copy.63 = f32[8,96,8,2,64]{4,3,2,1,0:T(2,128)} copy(f32[8,96,8,2,64]{1,2,3,0,4:T(8,128)} %fusion.49) | data formatting | bytes 6291456 | tf_op jit(solution)/shard_map/kmjc,srikj->scrim/transpose | solution.py:17
  251.5 7.1 %reshape.174 = f32[8,768,128]{2,1,0:T(8,128)} reshape(f32[8,96,8,2,64]{4,3,2,1,0:T(2,128)} %copy.63) | data formatting | bytes 6291456 | tf_op jit(solution)/shard_map/reshape | solution.py:93
  258.6 6.3 %all-to-all-start.3 = ((f32[8,768,128]{2,1,0:T(8,128)}), f32[8,768,128]{2,1,0:T(8,128)}, u32[]{:S(2)}, u32[]{:S(2)}) async-start(f32[8,768,128]{2,1,0:T(8,128)} %reshape.174), calls=%async_computation.3 | async-start | bytes 6291456 | tf_op jit(solution)/shard_map/all_to_all | solution.py:49
  264.9 10.4 %fusion.44 = f32[8,96,8,2,64]{1,2,3,0,4:T(8,128)} fusion(f32[8,8,2,64,2,1]{3,1,4,2,0,5:T(8,128)S(1)} %copy-done.5, f32[64,64,2,96,1,1]{3,1,2,0,5,4:T(8,128)} %get-tuple-element.8), kind=kOutput, calls=%fused_computation.56 | convolution fusion | flops 603979776 | bytes 6356992 | tf_op jit(solution)/shard_map/kmjc,srikj->scrim/dot_general | solution.py:17
  275.3 8.3 %copy.54 = f32[8,96,8,2,64]{4,3,2,1,0:T(2,128)} copy(f32[8,96,8,2,64]{1,2,3,0,4:T(8,128)} %fusion.44) | data formatting | bytes 6291456 | tf_op jit(solution)/shard_map/kmjc,srikj->scrim/transpose | solution.py:17
  283.6 7.1 %reshape.170 = f32[8,768,128]{2,1,0:T(8,128)} reshape(f32[8,96,8,2,64]{4,3,2,1,0:T(2,128)} %copy.54) | data formatting | bytes 6291456 | tf_op jit(solution)/shard_map/reshape | solution.py:93
  290.7 44.6 %all-to-all-done.3 = f32[8,768,128]{2,1,0:T(8,128)} async-done(((f32[8,768,128]{2,1,0:T(8,128)}), f32[8,768,128]{2,1,0:T(8,128)}, u32[]{:S(2)}, u32[]{:S(2)}) %all-to-all-start.3) | async-done | bytes 3145760 | tf_op jit(solution)/shard_map/all_to_all | solution.py:49
  335.2 4.5 %all-to-all-start.1 = ((f32[8,768,128]{2,1,0:T(8,128)}), f32[8,768,128]{2,1,0:T(8,128)}, u32[]{:S(2)}, u32[]{:S(2)}) async-start(f32[8,768,128]{2,1,0:T(8,128)} %reshape.170), calls=%async_computation.1 | async-start | bytes 6291456 | tf_op jit(solution)/shard_map/all_to_all | solution.py:49
  340.5 9.6 %fusion.97 = (f32[8,1024]{1,0:T(8,128)S(1)}, f32[8,1024]{1,0:T(8,128)S(1)}, f32[96,8,1024]{2,1,0:T(8,128)}) fusion(f32[8,1024]{1,0:T(8,128)S(1)} %get-tuple-element.20, f32[8,1024]{1,0:T(8,128)S(1)} %get-tuple-element.19, bf16[96,8,1024]{2,1,0:T(8,128)(2,1)S(1)} %copy-done.2, f32[96]{0:T(128)S(1)} %copy-done.11, f32[1024,8,128,1]{2,0,3,1:T(8,128)} %constant.49, ...), kind=kOutput, calls=%fused_computation.116 | convolution fusion | flops 4838899712 | bytes 13762944 | tf_op jit(solution)/shard_map/dcrq,ndq->crn/dot_general | solution.py:17
  352.1 57.8 %all-to-all-done.1 = f32[8,768,128]{2,1,0:T(8,128)} async-done(((f32[8,768,128]{2,1,0:T(8,128)}), f32[8,768,128]{2,1,0:T(8,128)}, u32[]{:S(2)}, u32[]{:S(2)}) %all-to-all-start.1) | async-done | bytes 3145760 | tf_op jit(solution)/shard_map/all_to_all | solution.py:49
  409.9 9.7 %fusion.39 = bf16[96,8,1024]{2,1,0:T(8,128)(2,1)} fusion(bf16[96,8,1024]{2,1,0:T(8,128)(2,1)S(1)} %copy-done.2, f32[96]{0:T(128)S(1)} %copy-done.14, f32[96]{0:T(128)S(1)} %copy-done.12, f32[8,1024]{1,0:T(8,128)S(1)} %get-tuple-element.20, f32[8,1024]{1,0:T(8,128)S(1)} %get-tuple-element.19, f32[1024,8,128,1]{2,0,3,1:T(8,128)} %constant.49, ...), kind=kOutput, calls=%fused_computation.49 | convolution fusion | flops 4838129664 | bytes 10552064 | tf_op jit(solution)/shard_map/dcrq,ndq->crn/dot_general | solution.py:17
  (64 shorter events, 14.0 us)
Async XLA Ops:
  10.8 7.5 %copy-start.2 = (bf16[96,8,1024]{2,1,0:T(8,128)(2,1)S(1)}, bf16[96,8,1024]{2,1,0:T(8,128)(2,1)}, u32[]{:S(2)}) copy-start(bf16[96,8,1024]{2,1,0:T(8,128)(2,1)} %param.10) | copy-start | bytes 4718596
  10.8 13.7 %copy-start.11 = (f32[96]{0:T(128)S(1)}, f32[96]{0:T(128)}, u32[]{:S(2)}) copy-start(f32[96]{0:T(128)} %param.12) | copy-start | bytes 1156
  10.9 13.7 %copy-start.13 = (f32[96]{0:T(128)S(1)}, f32[96]{0:T(128)}, u32[]{:S(2)}) copy-start(f32[96]{0:T(128)} %param.13) | copy-start | bytes 1156
  10.9 78.3 %all-to-all-start.2 = ((f32[8,768,128]{2,1,0:T(8,128)}), f32[8,768,128]{2,1,0:T(8,128)}, u32[]{:S(2)}, u32[]{:S(2)}) async-start(f32[8,768,128]{2,1,0:T(8,128)} %bitcast.220), calls=%async_computation.2 | async-start | bytes 6291456 | tf_op jit(solution)/shard_map/all_to_all | solution.py:49
  18.8 4.3 %collective-permute-start.1 = (f32[2,8,1024]{2,1,0:T(8,128)S(1)}, f32[2,8,1024]{2,1,0:T(8,128)S(1)}, u32[]{:S(2)}, u32[]{:S(2)}) collective-permute-start(f32[2,8,1024]{2,1,0:T(8,128)S(1)} %pad_maximum_fusion.2), channel_id=1, source_target_pairs={{0,2},{1,3},{2,0},{3,1},{4,6},{5,7},{6,4},{7,5},{8,10},{9,11},{10,... | collective-permute-start | bytes 196616 | tf_op jit(solution)/shard_map/ppermute | solution.py:44
  20.3 3.2 collective-permute-start.2
  20.3 4.2 collective-permute-start
  33.9 60.0 %copy-start.7 = (f32[1,2,96,96]{3,2,1,0:T(8,128)S(1)}, f32[1,2,96,96]{3,2,1,0:T(8,128)}, u32[]{:S(2)}) copy-start(f32[1,2,96,96]{3,2,1,0:T(8,128)} %param.14) | copy-start | bytes 221188
  33.9 60.0 %copy-start.8 = (f32[1,2,96,96]{3,2,1,0:T(8,128)S(1)}, f32[1,2,96,96]{3,2,1,0:T(8,128)}, u32[]{:S(2)}) copy-start(f32[1,2,96,96]{3,2,1,0:T(8,128)} %param.16) | copy-start | bytes 221188
  89.1 74.9 %all-to-all-start = ((f32[8,768,128]{2,1,0:T(8,128)}), f32[8,768,128]{2,1,0:T(8,128)}, u32[]{:S(2)}, u32[]{:S(2)}) async-start(f32[8,768,128]{2,1,0:T(8,128)} %bitcast.219), calls=%async_computation | async-start | bytes 6291456 | tf_op jit(solution)/shard_map/all_to_all | solution.py:49
  101.1 8.1 %copy-start.6 = (f32[8,8,2,64,2,1]{3,0,1,2,4,5:T(8,128)S(1)}, f32[8,8,2,64,2,1]{3,0,1,2,4,5:T(8,128)}, u32[]{:S(2)}) copy-start(f32[8,8,2,64,2,1]{3,0,1,2,4,5:T(8,128)} %constant.46) | copy-start | bytes 196612
  183.4 4.3 %copy-start.1 = (f32[96,64,64,2]{0,2,3,1:T(8,128)S(1)}, f32[96,64,64,2]{0,2,3,1:T(8,128)}, u32[]{:S(2)}) copy-start(f32[96,64,64,2]{0,2,3,1:T(8,128)} %convolution_bitcast_fusion) | copy-start | bytes 9437188
  183.4 4.3 %copy-start.9 = (f32[1,2,96]{2,1,0:T(2,128)S(1)}, f32[1,2,96]{2,1,0:T(2,128)}, u32[]{:S(2)}) copy-start(f32[1,2,96]{2,1,0:T(2,128)} %param.15) | copy-start | bytes 2308
  183.4 4.3 %copy-start.10 = (f32[1,2,96]{2,1,0:T(2,128)S(1)}, f32[1,2,96]{2,1,0:T(2,128)}, u32[]{:S(2)}) copy-start(f32[1,2,96]{2,1,0:T(2,128)} %param.17) | copy-start | bytes 2308
  211.8 7.0 %copy-start = (f32[64,64,2,96]{3,1,2,0:T(8,128)}, f32[64,64,2,96]{3,1,2,0:T(8,128)S(1)}, u32[]{:S(2)}) copy-start(f32[64,64,2,96]{3,1,2,0:T(8,128)S(1)} %bitcast_select_fusion) | copy-start | bytes 9437188
  219.8 17.4 %copy-start.5 = (f32[8,8,2,64,2,1]{3,1,4,2,0,5:T(8,128)S(1)}, f32[8,8,2,64,2,1]{3,1,4,2,0,5:T(8,128)}, u32[]{:S(2)}) copy-start(f32[8,8,2,64,2,1]{3,1,4,2,0,5:T(8,128)} %constant.48) | copy-start | bytes 196612
  233.5 25.1 %all-to-all-start.4 = ((f32[8,1,4608]{2,1,0:T(1,128)}), f32[8,1,4608]{2,1,0:T(1,128)S(1)}, u32[]{:S(2)}, u32[]{:S(2)}) async-start(f32[8,1,4608]{2,1,0:T(1,128)} %mul.114), calls=%async_computation.4 | async-start | bytes 294912 | tf_op jit(solution)/shard_map/all_to_all | solution.py:49
  258.6 76.7 %all-to-all-start.3 = ((f32[8,768,128]{2,1,0:T(8,128)}), f32[8,768,128]{2,1,0:T(8,128)}, u32[]{:S(2)}, u32[]{:S(2)}) async-start(f32[8,768,128]{2,1,0:T(8,128)} %reshape.174), calls=%async_computation.3 | async-start | bytes 6291456 | tf_op jit(solution)/shard_map/all_to_all | solution.py:49
  290.7 49.8 %copy-start.4 = (bf16[96,8,1024]{2,1,0:T(8,128)(2,1)S(1)}, bf16[96,8,1024]{2,1,0:T(8,128)(2,1)}, u32[]{:S(2)}) copy-start(bf16[96,8,1024]{2,1,0:T(8,128)(2,1)} %param.11) | copy-start | bytes 4718596
  335.2 74.7 %all-to-all-start.1 = ((f32[8,768,128]{2,1,0:T(8,128)}), f32[8,768,128]{2,1,0:T(8,128)}, u32[]{:S(2)}, u32[]{:S(2)}) async-start(f32[8,768,128]{2,1,0:T(8,128)} %reshape.170), calls=%async_computation.1 | async-start | bytes 6291456 | tf_op jit(solution)/shard_map/all_to_all | solution.py:49
  340.5 69.4 %copy-start.12 = (f32[96]{0:T(128)S(1)}, f32[96]{0:T(128)}, u32[]{:S(2)}) copy-start(f32[96]{0:T(128)} %param.12) | copy-start | bytes 1156
  340.5 69.4 %copy-start.14 = (f32[96]{0:T(128)S(1)}, f32[96]{0:T(128)}, u32[]{:S(2)}) copy-start(f32[96]{0:T(128)} %param.13) | copy-start | bytes 1156
  350.0 69.6 %collective-permute-start.4 = (f32[2,8,1024]{2,1,0:T(8,128)S(1)}, f32[2,8,1024]{2,1,0:T(8,128)S(1)}, u32[]{:S(2)}, u32[]{:S(2)}) collective-permute-start(f32[2,8,1024]{2,1,0:T(8,128)S(1)} %pad_maximum_fusion.3), channel_id=1, source_target_pairs={{0,2},{1,3},{2,0},{3,1},{4,6},{5,7},{6,4},{7,5},{8,10},{9,11},{10,... | collective-permute-start | bytes 196616 | tf_op jit(solution)/shard_map/ppermute | solution.py:44
  351.6 68.0 %collective-permute-start.5 = (f32[2,8,1024]{2,1,0:T(8,128)S(1)}, f32[2,8,1024]{2,1,0:T(8,128)S(1)}, u32[]{:S(2)}, u32[]{:S(2)}) collective-permute-start(f32[2,8,1024]{2,1,0:T(8,128)S(1)} %pad_maximum_fusion.3), channel_id=1, source_target_pairs={{0,3},{1,0},{2,1},{3,2},{4,7},{5,4},{6,5},{7,6},{8,11},{9,8},{10,9... | collective-permute-start | bytes 196616 | tf_op jit(solution)/shard_map/ppermute | solution.py:44
  351.6 68.1 %collective-permute-start.3 = (f32[2,8,1024]{2,1,0:T(8,128)S(1)}, f32[2,8,1024]{2,1,0:T(8,128)S(1)}, u32[]{:S(2)}, u32[]{:S(2)}) collective-permute-start(f32[2,8,1024]{2,1,0:T(8,128)S(1)} %pad_maximum_fusion.3), channel_id=1, source_target_pairs={{0,1},{1,2},{2,3},{3,0},{4,5},{5,6},{6,7},{7,4},{8,9},{9,10},{10,1... | collective-permute-start | bytes 196616 | tf_op jit(solution)/shard_map/ppermute | solution.py:44
  409.9 9.8 %copy-start.3 = (f32[96,8,1024]{2,1,0:T(8,128)S(1)}, f32[96,8,1024]{2,1,0:T(8,128)}, u32[]{:S(2)}) copy-start(f32[96,8,1024]{2,1,0:T(8,128)} %get-tuple-element.25) | copy-start | bytes 9437188
